TPU v7x, 512 devices: a whole 4x8x8 slice. The times are simulated.
512 devices in a mesh: samp: 32 (over x, y_lo, core), var: 16 (over z, y_hi).
Axes of the slice: x: 4, y: 8 (y_hi: 2, y_lo: 4; y = y_hi * 4 + y_lo), z: 8, core: 2. Of those that a mesh axis runs over, the one named last changes fastest.
Arguments:
- genotypes: bfloat16 [16384, 40960], P('samp', 'var'), may hold values from 0 to 2, as said below
- imputed: bfloat16 [16384, 20480], P('samp', 'var'), may hold values from 0 to 2, as said below
- centre: int32 [16384], P('samp'), may hold values from 0 to 21, as said below
- phenotypes: float32 [8, 16384], P(None, 'samp'), may hold values from -6 to 6
- earlier: float32 [8, 16384], P(None, 'samp'), may hold values from -6 to 6
- genetic: float32 [8], replicated, may hold values from 0.2 to 2
- noise: float32 [8], replicated, may hold values from 0.2 to 2
Outputs:
- solution: float32 [8, 16384], P(None, ('samp', 'var'))
- residual: float32 [8, 16384], P(None, ('samp', 'var'))
- scores: float32 [8, 20480], P(None, 'var')
Inputs may be any that keep to these rules, and one draw needn't show every extreme that they name: `genotypes`: allele dosages 0, 1 or 2; every variant has its own allele frequency. `imputed`: allele dosages 0, 1 or 2; every variant has its own allele frequency. One of 22 centres; a centre may have no samples.
All inputs are finite; a program needn't handle non-finite values.
Results may differ from a plain program's by a relative error of at most 0.033.
Values may be sent and summed in bfloat16 or wider, within the bound.
No kernel may reach another device: no remote copies, remote signals or barrier semaphores. Data moves between devices by JAX's collectives and lax.ppermute only.
A program may use at most 64 MiB of HBM per device.

v0:
```python
import jax
import jax.numpy as jnp
from jax import lax
from jax.sharding import PartitionSpec as P

M = 40960
CENTRES = 22
ITERS = 2


def inner(values):
    return lax.psum((values[0],), "samp")


def operate(direction, standard, genetic, noise):
    low = direction.astype(jnp.bfloat16)
    partial_proj = jnp.dot(low, standard, preferred_element_type=jnp.float32)
    scale_row = (genetic / M)[:, None]
    summed_proj = lax.psum(partial_proj, "samp")
    scaled = (summed_proj * scale_row).astype(jnp.bfloat16)
    partial_back = lax.dot_general(
        scaled, standard, (((1,), (1,)), ((), ())), preferred_element_type=jnp.float32
    )
    back = lax.psum(partial_back, "var")
    return back + noise[:, None] * direction


def shards(genotypes, imputed, centre, phenotypes, earlier, genetic, noise):
    rows = genotypes.shape[0]
    total = rows * lax.axis_size("samp")
    share = rows // lax.axis_size("var")
    offset = lax.axis_index("var") * share
    values = genotypes.astype(jnp.float32)
    dosage = imputed.astype(jnp.float32)
    onehot = (centre[:, None] == jnp.arange(CENTRES, dtype=jnp.int32)[None, :]).astype(jnp.float32)
    sums = lax.psum(
        (
            jnp.sum(values, axis=0),
            jnp.sum(values * values, axis=0),
            jnp.sum(dosage, axis=0),
            jnp.sum(dosage * dosage, axis=0),
            jnp.dot(earlier, dosage, precision=lax.Precision.HIGHEST),
            jnp.dot(phenotypes, onehot, precision=lax.Precision.HIGHEST),
            jnp.sum(onehot, axis=0),
            jnp.sum(earlier, axis=1),
            jnp.sum(earlier * earlier, axis=1),
        ),
        "samp",
    )
    gen_sum, gen_sq, imp_sum, imp_sq, imp_cross, centre_sum, counts, earlier_sum, earlier_sq = sums
    mean_col = gen_sum / total
    var_col = gen_sq / total - mean_col * mean_col
    standard = ((values - mean_col[None, :]) * lax.rsqrt(var_col + 1e-05)[None, :]).astype(
        jnp.bfloat16
    )
    imp_mean = imp_sum / total
    imp_var = imp_sq / total - imp_mean * imp_mean + 1e-05
    earlier_var = earlier_sq / total + 1e-05
    cross = imp_cross - earlier_sum[:, None] * imp_mean[None, :]
    scores = cross / jnp.sqrt(total * imp_var[None, :] * earlier_var[:, None])
    centre_mean = centre_sum / jnp.maximum(counts, 1.0)[None, :]
    centred = phenotypes - jnp.dot(centre_mean, onehot.T, precision=lax.Precision.HIGHEST)
    solution = jnp.zeros_like(centred)
    residual = centred
    direction = residual
    (norm_now,) = inner((jnp.sum(residual * residual, axis=1),))
    for step in range(ITERS):
        image = operate(direction, standard, genetic, noise)
        (curve,) = inner((jnp.sum(direction * image, axis=1),))
        alpha = norm_now / curve
        solution = solution + alpha[:, None] * direction
        residual = residual - alpha[:, None] * image
        if step + 1 < ITERS:
            (norm_next,) = inner((jnp.sum(residual * residual, axis=1),))
            direction = residual + (norm_next / norm_now)[:, None] * direction
            norm_now = norm_next
    solution = lax.dynamic_slice_in_dim(solution, offset, share, 1)
    residual = lax.dynamic_slice_in_dim(residual, offset, share, 1)
    return (solution, residual, scores)


def solution(mesh):
    in_specs = (
        P("samp", "var"),
        P("samp", "var"),
        P("samp"),
        P(None, "samp"),
        P(None, "samp"),
        P(),
        P(),
    )
    out_specs = (P(None, ("samp", "var")), P(None, ("samp", "var")), P(None, "var"))
    return jax.shard_map(shards, mesh=mesh, in_specs=in_specs, out_specs=out_specs, check_vma=False)
```

profile of v0, /device:TPU:64, one launch (start us, length us, event | category | flops | bytes accessed | tf_op | source)
XLA Modules:
  0.0 1123.9 jit_solution(7656716114734789581)
XLA Ops:
  7.2 2.5 convert_reduce_fusion
  9.8 0.1 convert_reduce_fusion.2
  9.9 0.1 convolution_bitcast_fusion
  10.1 138.6 %all-reduce.2 = (f32[8,22]{0,1:T(8,128)S(1)}, f32[22]{0:T(128)S(1)}, f32[2560]{0:T(1024)S(1)}, f32[2560]{0:T(1024)S(1)}) all-reduce(f32[8,22]{0,1:T(8,128)S(1)} %convolution_bitcast_fusion, f32[22]{0:T(128)S(1)} %convert_reduce_fusion.2, f32[2560]{0:T(1024)S(1)} %get-tuple-element.4, ...), channel_id=1, replica_groups=mesh['samp'=32,'var'=16] {'samp'}, use_global_device_ids=true, to_apply=%region_0.0 | all-reduce | flops 5318 | bytes 42544 | tf_op jit(solution)/shard_map/psum | solution.py:36
  148.7 0.3 convolution_subtract_fusion
  149.0 3.1 fusion.10
  152.2 0.6 fusion.22
  152.8 0.4 convert_reduce_fusion.1
  153.2 248.6 %all-reduce.6.cloned.1.call-done = f32[8,2560]{1,0:T(8,128)} async-done(((f32[8,2560]{1,0:T(8,128)}), f32[8,2560]{1,0:T(8,128)}) %all-reduce.6.cloned.1.call-update) | async-done | bytes 81936 | tf_op jit(solution)/shard_map/psum | solution.py:19
  401.7 2.6 fusion.8
  404.3 97.8 %psum.125 = f32[8,512]{1,0:T(8,128)S(1)} all-reduce(f32[8,512]{1,0:T(8,128)S(1)} %fusion.8), channel_id=1, replica_groups=mesh['samp'=32,'var'=16] {'var'}, use_global_device_ids=true, to_apply=%region_10.0 | all-reduce | flops 4096 | bytes 32768 | tf_op jit(solution)/shard_map/psum | solution.py:24
  502.2 0.2 multiply_reduce_fusion.3
  502.3 67.4 %all-reduce.1 = (f32[8]{0:T(128)S(1)}, f32[8]{0:T(128)S(1)}) all-reduce(f32[8]{0:T(128)S(1)} %get-tuple-element.10, f32[8]{0:T(128)S(1)} %get-tuple-element.9), channel_id=1, replica_groups=mesh['samp'=32,'var'=16] {'samp'}, use_global_device_ids=true, to_apply=%region_4.0 | all-reduce | flops 16 | bytes 128 | tf_op jit(solution)/shard_map/psum | solution.py:12
  569.7 0.2 multiply_reduce_fusion.2
  569.9 67.4 %psum.127 = f32[8]{0:T(128)S(1)} all-reduce(f32[8]{0:T(128)S(1)} %get-tuple-element.25), channel_id=1, replica_groups=mesh['samp'=32,'var'=16] {'samp'}, use_global_device_ids=true, to_apply=%region_14.0 | all-reduce | flops 8 | bytes 64 | tf_op jit(solution)/shard_map/psum | solution.py:12
  637.4 1.3 fusion.6
  638.7 0.1 fusion.21
  638.9 243.8 %all-reduce.8.cloned.1.call-done = f32[8,2560]{1,0:T(8,128)} async-done(((f32[8,2560]{1,0:T(8,128)}), f32[8,2560]{1,0:T(8,128)}) %all-reduce.8.cloned.1.call-update) | async-done | bytes 81936 | tf_op jit(solution)/shard_map/psum | solution.py:19
  882.6 1.7 fusion.4
  884.3 97.8 %psum.129 = f32[8,512]{1,0:T(8,128)S(1)} all-reduce(f32[8,512]{1,0:T(8,128)S(1)} %fusion.4), channel_id=1, replica_groups=mesh['samp'=32,'var'=16] {'var'}, use_global_device_ids=true, to_apply=%region_16.0 | all-reduce | flops 4096 | bytes 32768 | tf_op jit(solution)/shard_map/psum | solution.py:24
  982.2 0.2 multiply_reduce_fusion.1
  982.3 133.3 %all-reduce = (f32[8]{0:T(128)S(1)}, f32[8,1280]{1,0:T(8,128)S(1)}, f32[8]{0:T(128)S(1)}, f32[1280]{0:T(1024)S(1)}, f32[1280]{0:T(1024)S(1)}, /*index=5*/f32[8]{0:T(128)S(1)}) all-reduce(f32[8]{0:T(128)S(1)} %get-tuple-element.23, f32[8,1280]{1,0:T(8,128)S(1)} %fusion.22, ...), channel_id=1, replica_groups=mesh['samp'=32,'var'=16] {'samp'}, use_global_device_ids=true, to_apply=%region_18.0 | all-reduce | flops 12824 | bytes 102592 | tf_op jit(solution)/shard_map/psum | solution.py:12
  1115.7 0.7 dynamic-slice_subtract_fusion
  1116.3 0.7 rsqrt_multiply_fusion
  (27 shorter events, 0.3 us)
Async XLA Ops:
  7.2 2.6 copy-start.4
  7.2 2.7 copy-start.3
  7.2 394.6 %all-reduce.6.cloned.1.call-start = ((), (), s32[]{:S(2)}) async-start(), calls=%async_computation | async-start | bytes 163840 | tf_op jit(solution)/shard_map/psum | solution.py:19
  9.8 142.3 %copy-start.6 = (f32[8]{0:T(128)S(1)}, f32[8]{0:T(128)}, u32[]{:S(2)}) copy-start(f32[8]{0:T(128)} %param.12) | copy-start | bytes 100
  9.8 142.4 %copy-start = (bf16[512,1280]{1,0:T(8,128)(2,1)S(1)}, bf16[512,1280]{1,0:T(8,128)(2,1)}, u32[]{:S(2)}) copy-start(bf16[512,1280]{1,0:T(8,128)(2,1)} %param.8) | copy-start | bytes 3932164
  9.8 142.4 %copy-start.2 = (f32[8,512]{1,0:T(8,128)S(1)}, f32[8,512]{1,0:T(8,128)}, u32[]{:S(2)}) copy-start(f32[8,512]{1,0:T(8,128)} %param.11) | copy-start | bytes 49156
  152.1 730.6 %all-reduce.8.cloned.1.call-start = ((), (), s32[]{:S(2)}) async-start(), calls=%async_computation.1 | async-start | bytes 163840 | tf_op jit(solution)/shard_map/psum | solution.py:19
  152.8 349.4 %copy-start.5 = (f32[8]{0:T(128)S(1)}, f32[8]{0:T(128)}, u32[]{:S(2)}) copy-start(f32[8]{0:T(128)} %param.13) | copy-start | bytes 100
  153.2 484.2 %copy-start.1 = (bf16[512,2560]{1,0:T(8,128)(2,1)S(1)}, bf16[512,2560]{1,0:T(8,128)(2,1)}, u32[]{:S(2)}) copy-start(bf16[512,2560]{1,0:T(8,128)(2,1)} %param.7) | copy-start | bytes 7864324
Sparse Core Ops, SparseCore 0:
  152.2 249.5 all-reduce.5
  638.8 243.7 all-reduce.7
where the time goes:
time: 1120 us
  blocking collectives  602 us (54%)
  waiting for transfers between devices  492 us (44%)
  between operations  14.2 us (1%)
    psum x2, waiting for transfers between devices, operate(): summed_proj = lax.psum(partial_proj, 'samp')  492 us
    psum x3, blocking collectives, inner(): return lax.psum((values[0],), 'samp')  268 us
    psum x2, blocking collectives, operate(): back = lax.psum(partial_back, 'var')  196 us
    psum x1, blocking collectives, shards(): lax.psum((jnp.sum(values, axis=0), jnp.sum(values * values, axis=0), jnp....  139 us
  transfers between devices with their start and end apart: 2, of which 2 were waited for; matrix products, arithmetic and copies ran while one was open for 0% of the time, Pallas kernels for 0%

commit v1 on v0

--- a/solution.py
+++ b/solution.py
@@ -16,7 +16,7 @@
     low = direction.astype(jnp.bfloat16)
     partial_proj = jnp.dot(low, standard, preferred_element_type=jnp.float32)
     scale_row = (genetic / M)[:, None]
-    summed_proj = lax.psum(partial_proj, "samp")
+    summed_proj = jnp.sum(lax.all_gather(partial_proj, "samp"), axis=0)
     scaled = (summed_proj * scale_row).astype(jnp.bfloat16)
     partial_back = lax.dot_general(
         scaled, standard, (((1,), (1,)), ((), ())), preferred_element_type=jnp.float32

time: 1120 us -> 750 us (0.67)
  waiting for transfers between devices: 492 us -> 118 us
    psum x2 -> x0, waiting for transfers between devices: 492 us -> none  [operate(): summed_proj = lax.psum(partial_proj, 'samp')]
    all_gather x0 -> x2, waiting for transfers between devices: none -> 118 us  [operate(): summed_proj = jnp.sum(lax.all_gather(partial_proj, 'samp'), axis=0)]
where the time goes in v1:
time: 750 us
  blocking collectives  600 us (80%)
  waiting for transfers between devices  118 us (16%)
  between operations  14.2 us (2%)
  other arithmetic  9.13 us (1%)
  matrix products  8.76 us (1%)
    psum x3, blocking collectives, inner(): return lax.psum((values[0],), 'samp')  268 us
    psum x2, blocking collectives, operate(): back = lax.psum(partial_back, 'var')  193 us
    psum x1, blocking collectives, shards(): lax.psum((jnp.sum(values, axis=0), jnp.sum(values * values, axis=0), jnp....  138 us
    all_gather x2, waiting for transfers between devices, operate(): summed_proj = jnp.sum(lax.all_gather(partial_proj, 'samp'), axis=0)  118 us
  transfers between devices with their start and end apart: 2, of which 2 were waited for; matrix products, arithmetic and copies ran while one was open for 0% of the time, Pallas kernels for 0%

profile of v1, /device:TPU:64, one launch (start us, length us, event | category | flops | bytes accessed | tf_op | source)
XLA Modules:
  0.0 750.1 jit_solution(793936042653474028)
XLA Ops:
  7.2 2.7 convert_reduce_fusion
  10.2 138.5 %all-reduce.2 = (f32[8,22]{0,1:T(8,128)S(1)}, f32[22]{0:T(128)S(1)}, f32[2560]{0:T(1024)S(1)}, f32[2560]{0:T(1024)S(1)}) all-reduce(f32[8,22]{0,1:T(8,128)S(1)} %convolution_bitcast_fusion, f32[22]{0:T(128)S(1)} %convert_reduce_fusion.2, f32[2560]{0:T(1024)S(1)} %get-tuple-element.4, ...), channel_id=1, replica_groups=mesh['samp'=32,'var'=16] {'samp'}, use_global_device_ids=true, to_apply=%region_0.0 | all-reduce | flops 5318 | bytes 42544 | tf_op jit(solution)/shard_map/psum | solution.py:36
  148.7 0.3 convolution_subtract_fusion
  149.0 1.3 fusion.10
  150.4 62.3 %all-gather.5.cloned.1.call-done = f32[256,2560]{1,0:T(8,128)} async-done(((f32[8,2560]{1,0:T(8,128)}), f32[256,2560]{1,0:T(8,128)}) %all-gather.5.cloned.1.call-update) | async-done | bytes 2621456 | tf_op jit(solution)/shard_map/all_gather | solution.py:19
  212.8 1.9 bitcast_reduce_fusion.1
  214.6 0.8 fusion.8
  215.4 96.8 %psum.110 = f32[8,512]{1,0:T(8,128)S(1)} all-reduce(f32[8,512]{1,0:T(8,128)S(1)} %fusion.8), channel_id=1, replica_groups=mesh['samp'=32,'var'=16] {'var'}, use_global_device_ids=true, to_apply=%region_10.0 | all-reduce | flops 4096 | bytes 32768 | tf_op jit(solution)/shard_map/psum | solution.py:24
  312.2 0.2 multiply_reduce_fusion.3
  312.4 67.5 %all-reduce.1 = (f32[8]{0:T(128)S(1)}, f32[8]{0:T(128)S(1)}) all-reduce(f32[8]{0:T(128)S(1)} %get-tuple-element.10, f32[8]{0:T(128)S(1)} %get-tuple-element.9), channel_id=1, replica_groups=mesh['samp'=32,'var'=16] {'samp'}, use_global_device_ids=true, to_apply=%region_4.0 | all-reduce | flops 16 | bytes 128 | tf_op jit(solution)/shard_map/psum | solution.py:12
  379.9 0.2 multiply_reduce_fusion.2
  380.1 67.4 %psum.112 = f32[8]{0:T(128)S(1)} all-reduce(f32[8]{0:T(128)S(1)} %get-tuple-element.25), channel_id=1, replica_groups=mesh['samp'=32,'var'=16] {'samp'}, use_global_device_ids=true, to_apply=%region_14.0 | all-reduce | flops 8 | bytes 64 | tf_op jit(solution)/shard_map/psum | solution.py:12
  447.5 3.1 fusion.6
  450.7 0.1 fusion.21
  450.8 0.4 convert_reduce_fusion.1
  451.2 0.6 fusion.22
  451.8 55.5 %all-gather.7.cloned.1.call-done = f32[256,2560]{1,0:T(8,128)} async-done(((f32[8,2560]{1,0:T(8,128)}), f32[256,2560]{1,0:T(8,128)}) %all-gather.7.cloned.1.call-update) | async-done | bytes 2621456 | tf_op jit(solution)/shard_map/all_gather | solution.py:19
  507.3 1.9 bitcast_reduce_fusion
  509.2 2.5 fusion.4
  511.7 96.7 %psum.113 = f32[8,512]{1,0:T(8,128)S(1)} all-reduce(f32[8,512]{1,0:T(8,128)S(1)} %fusion.4), channel_id=1, replica_groups=mesh['samp'=32,'var'=16] {'var'}, use_global_device_ids=true, to_apply=%region_16.0 | all-reduce | flops 4096 | bytes 32768 | tf_op jit(solution)/shard_map/psum | solution.py:24
  608.4 0.2 multiply_reduce_fusion.1
  608.5 133.3 %all-reduce = (f32[8]{0:T(128)S(1)}, f32[8,1280]{1,0:T(8,128)S(1)}, f32[8]{0:T(128)S(1)}, f32[1280]{0:T(1024)S(1)}, f32[1280]{0:T(1024)S(1)}, /*index=5*/f32[8]{0:T(128)S(1)}) all-reduce(f32[8]{0:T(128)S(1)} %get-tuple-element.23, f32[8,1280]{1,0:T(8,128)S(1)} %fusion.22, ...), channel_id=1, replica_groups=mesh['samp'=32,'var'=16] {'samp'}, use_global_device_ids=true, to_apply=%region_18.0 | all-reduce | flops 12824 | bytes 102592 | tf_op jit(solution)/shard_map/psum | solution.py:12
  741.9 0.7 dynamic-slice_subtract_fusion
  742.5 0.7 rsqrt_multiply_fusion
  (29 shorter events, 0.5 us)
Async XLA Ops:
  7.2 141.8 %copy-start.1 = (bf16[512,2560]{1,0:T(8,128)(2,1)S(1)}, bf16[512,2560]{1,0:T(8,128)(2,1)}, u32[]{:S(2)}) copy-start(bf16[512,2560]{1,0:T(8,128)(2,1)} %param.7) | copy-start | bytes 7864324
  7.2 2.7 copy-start.4
  7.2 2.9 copy-start.3
  7.2 205.6 %all-gather.5.cloned.1.call-start = ((), (), s32[]{:S(2)}) async-start(), calls=%async_computation | async-start | bytes 2703360 | tf_op jit(solution)/shard_map/all_gather | solution.py:19
  9.9 140.5 %copy-start.6 = (f32[8]{0:T(128)S(1)}, f32[8]{0:T(128)}, u32[]{:S(2)}) copy-start(f32[8]{0:T(128)} %param.12) | copy-start | bytes 100
  150.3 356.9 %all-gather.7.cloned.1.call-start = ((), (), s32[]{:S(2)}) async-start(), calls=%async_computation.1 | async-start | bytes 2703360 | tf_op jit(solution)/shard_map/all_gather | solution.py:19
  150.4 161.8 %copy-start.5 = (f32[8]{0:T(128)S(1)}, f32[8]{0:T(128)}, u32[]{:S(2)}) copy-start(f32[8]{0:T(128)} %param.13) | copy-start | bytes 100
  215.4 235.2 %copy-start.2 = (f32[8,512]{1,0:T(8,128)S(1)}, f32[8,512]{1,0:T(8,128)}, u32[]{:S(2)}) copy-start(f32[8,512]{1,0:T(8,128)} %param.11) | copy-start | bytes 49156
  215.4 235.4 %copy-start = (bf16[512,1280]{1,0:T(8,128)(2,1)S(1)}, bf16[512,1280]{1,0:T(8,128)(2,1)}, u32[]{:S(2)}) copy-start(bf16[512,1280]{1,0:T(8,128)(2,1)} %param.8) | copy-start | bytes 3932164
Sparse Core Ops, SparseCore 0:
  150.5 62.2 all-gather.4
  450.8 56.4 all-gather.6
